TPU v7x, 128 devices: a whole 4x4x4 slice. The times are simulated.
128 devices in a mesh: seq: 16 (over x_lo, y, core), heads: 8 (over z, x_hi).
Axes of the slice: x: 4 (x_hi: 2, x_lo: 2; x = x_hi * 2 + x_lo), y: 4, z: 4, core: 2. Of those that a mesh axis runs over, the one named last changes fastest.
Arguments:
- hidden_in: bfloat16 [4096, 8192], P('seq', 'heads'), may hold values from -6 to 6
- queries: bfloat16 [4096, 8192], P('seq', 'heads'), as said below
- image_kv: bfloat16 [16, 2, 6528, 1024], P('seq', None, None, 'heads'), as said below
- out_weight: bfloat16 [8192, 8192], P('seq', 'heads'), may hold values from -0.0625 to 0.0625
- gate: float32 [1], replicated, may hold values from 0.4 to 1.2
- tile_counts: int32 [16], replicated, may hold values from 1 to 4, as said below
- owners: int32 [256], replicated, may hold values from 0 to 15, as said below
- starts: int32 [256], replicated, may hold values from 0 to 3, as said below
- norm_gain: float32 [8192], P('heads'), may hold values from 0.1 to 1.9
- norm_grad: bfloat16 [4096, 8192], P('seq', 'heads'), may hold values from -6 to 6
- stream_grad: bfloat16 [4096, 8192], P('seq', 'heads'), may hold values from -6 to 6
Outputs:
- hidden_out: bfloat16 [4096, 8192], P('seq', 'heads')
- stream_in_grad: float32 [4096, 8192], P('seq', 'heads')
Inputs may be any that keep to these rules, and one draw needn't show every extreme that they name: `tile_counts`: tiles of each image; some image has 4 tiles in every draw. `owners`: the image (named by the seq index that owns it) that a block of 16 text rows attends to; of the 16 blocks of one seq index at most 2 name the same image, and in every draw some image is named by exactly 2 blocks of every seq index. `starts`: the first tile a block sees, below the tile count of the block's image; in every draw some block starts at tile 0 and some at tile 4 - 1. `image_kv`: keys and values are real-valued. real-valued queries.
All inputs are finite; a program needn't handle non-finite values.
Results may differ from a plain program's by a relative error of at most 0.007.
Values may be sent and summed in bfloat16 or wider, within the bound.
No kernel may reach another device: no remote copies, remote signals or barrier semaphores. Data moves between devices by JAX's collectives and lax.ppermute only.
A program may use at most 128 MiB of HBM per device.

v0:
```python
import math
import jax
import jax.numpy as jnp
from jax import lax
from jax.sharding import PartitionSpec as P

D = 8192
HEAD_DIM = 128
TILE_TOK = 1601
BLOCKS_DEV = 16
CAP = 2
BLK = 16
EPS = 1e-05


def head_scores(query_head, key_block, scale):
    return (
        lax.dot_general(
            query_head, key_block, (((1,), (1,)), ((), ())), preferred_element_type=jnp.float32
        )
        * scale
    )


def local(
    hidden_in,
    queries,
    image_kv,
    out_weight,
    gate,
    tile_counts,
    owners,
    starts,
    norm_gain,
    norm_grad,
    stream_grad,
):
    seq_count = lax.axis_size("seq")
    here = lax.axis_index("seq")
    tok_rows, q_width = queries.shape
    q_heads = q_width // HEAD_DIM
    slot_count = seq_count * CAP
    scale = 1.0 / math.sqrt(HEAD_DIM)
    owner_table = owners.reshape(seq_count, BLOCKS_DEV)
    start_table = starts.reshape(seq_count, BLOCKS_DEV)
    my_owner = lax.dynamic_index_in_dim(owner_table, here, 0, keepdims=False)
    block_ids = jnp.arange(BLOCKS_DEV)
    same = my_owner[:, None] == my_owner[None, :]
    earlier = block_ids[None, :] < block_ids[:, None]
    my_rank = jnp.sum(jnp.logical_and(same, earlier).astype(jnp.int32), axis=1)
    my_slot = my_owner * CAP + my_rank
    placing = (my_slot[:, None] == jnp.arange(slot_count)[None, :]).astype(jnp.bfloat16)
    q_blocks = queries.reshape(BLOCKS_DEV, BLK, q_width)
    outgoing = jnp.einsum(
        "bs,brc->src", placing, q_blocks, preferred_element_type=jnp.float32
    ).astype(jnp.bfloat16)
    outgoing = outgoing.reshape(seq_count, CAP, BLK, q_width)
    arriving = owner_table == here
    arrive_rank = jnp.cumsum(arriving.astype(jnp.int32), axis=1) - 1
    slot_hit = jnp.logical_and(
        arriving[:, :, None], arrive_rank[:, :, None] == jnp.arange(CAP)[None, None, :]
    )
    slot_start = jnp.sum(jnp.where(slot_hit, start_table[:, :, None], 0), axis=1)
    tile_here = lax.dynamic_index_in_dim(tile_counts, here, 0, keepdims=False)
    key_end = tile_here * TILE_TOK
    keys_here = image_kv[0, 0]
    values_here = image_kv[0, 1]
    received = lax.all_to_all(outgoing, "seq", split_axis=0, concat_axis=0, tiled=True)
    flat = received.reshape(-1, q_width)
    row_first = jnp.broadcast_to(slot_start[:, :, None], received.shape[:3]).reshape(-1) * TILE_TOK

    def one_head(head):
        query_head = lax.dynamic_slice_in_dim(flat, head * HEAD_DIM, HEAD_DIM, 1)
        spot = jnp.arange(keys_here.shape[0])
        seen = jnp.logical_and(spot[None, :] >= row_first[:, None], spot[None, :] < key_end)
        scores = jnp.where(seen, head_scores(query_head, keys_here, scale), -jnp.inf)
        highest = jnp.max(scores, axis=1, keepdims=True)
        probs = jnp.exp(scores - highest)
        total = jnp.sum(probs, axis=1, keepdims=True)
        mixed = jnp.dot(probs.astype(jnp.bfloat16), values_here, preferred_element_type=jnp.float32)
        return (mixed / total).astype(jnp.bfloat16)

    heads_out = lax.map(one_head, jnp.arange(q_heads))
    merged = jnp.moveaxis(heads_out, 0, 1).reshape(received.shape)
    returned = lax.all_to_all(merged, "seq", split_axis=0, concat_axis=0, tiled=True)
    context = jnp.einsum(
        "bs,src->brc",
        placing,
        returned.reshape(slot_count, BLK, q_width),
        preferred_element_type=jnp.float32,
    )
    context = context.astype(jnp.bfloat16).reshape(tok_rows, q_width)
    full_context = lax.all_gather(context, "heads", axis=1, tiled=True)
    branch = jnp.dot(
        full_context,
        lax.all_gather(out_weight, "seq", axis=0, tiled=True),
        preferred_element_type=jnp.float32,
    )
    hidden_out = (hidden_in.astype(jnp.float32) + jnp.tanh(gate[0]) * branch).astype(jnp.bfloat16)
    hidden = hidden_out.astype(jnp.float32)
    scaled = norm_gain[None, :] * norm_grad.astype(jnp.float32)
    squares, product = lax.psum(
        (jnp.sum(hidden * hidden, axis=1), jnp.sum(hidden * scaled, axis=1)), "heads"
    )
    inverse = lax.rsqrt(squares / D + EPS)[:, None]
    project = (product / D)[:, None]
    stream_in_grad = (
        stream_grad.astype(jnp.float32) + inverse * scaled - inverse**3 * project * hidden
    )
    return (hidden_out, stream_in_grad)


def solution(mesh):
    placed = (
        P("seq", "heads"),
        P("seq", "heads"),
        P("seq", None, None, "heads"),
        P("seq", "heads"),
        P(),
        P(),
        P(),
        P(),
        P("heads"),
        P("seq", "heads"),
        P("seq", "heads"),
    )
    return jax.shard_map(
        local,
        mesh=mesh,
        in_specs=placed,
        out_specs=(P("seq", "heads"), P("seq", "heads")),
        check_vma=False,
    )
```

profile of v0, /device:TPU:0, one launch (start us, length us, event | category | flops | bytes accessed | tf_op | source)
XLA Modules:
  0.0 361.5 jit_solution(7062695272086445816)
XLA Ops:
  7.2 0.8 reshape.76
  9.3 2.0 copy.36
  11.2 5.7 %all-to-all-start = ((bf16[16,2,16,1024]{3,1,2,0:T(2,128)(2,1)}), bf16[16,2,16,1024]{3,1,2,0:T(2,128)(2,1)}, u32[]{:S(2)}, u32[]{:S(2)}) async-start(bf16[16,2,16,1024]{3,1,2,0:T(2,128)(2,1)} %copy.36), calls=%async_computation | async-start | bytes 2097152 | tf_op jit(solution)/shard_map/all_to_all | solution.py:68
  18.6 3.4 slice_bitcast_fusion
  21.9 11.6 %all-to-all-done = bf16[16,2,16,1024]{3,1,2,0:T(2,128)(2,1)} async-done(((bf16[16,2,16,1024]{3,1,2,0:T(2,128)(2,1)}), bf16[16,2,16,1024]{3,1,2,0:T(2,128)(2,1)}, u32[]{:S(2)}, u32[]{:S(2)}) %all-to-all-start) | async-done | bytes 1048608 | tf_op jit(solution)/shard_map/all_to_all | solution.py:68
  33.5 2.5 copy.37
  36.0 95.0 %while.11 = (s32[]{:T(128)}, bf16[8,512,128]{2,1,0:T(8,128)(2,1)}, s32[]{:T(128)}, s32[8]{0:T(128)S(1)}, bf16[512,1024]{1,0:T(8,128)(2,1)}, /*index=5*/bf16[6528...) while((s32[]{:T(128)}, bf16[8,512,128]{2,1,0:T(8,128)(2,1)}, ...), condition=%wide.region_6.7_spmd.clone, body=%wide.region_3.6_spmd.clone.sunk | while | flops 1741493632 | bytes 43744824 | solution.py:83
  36.0 0.6 dynamic_slice.29
  37.5 5.6 %fusion.52 = (f32[512]{0:T(512)S(1)}, f32[512,6528]{1,0:T(8,128)S(1)}) fusion(bf16[6528,128]{1,0:T(8,128)(2,1)} %get-tuple-element.183, bf16[512,1024]{1,0:T(8,128)(2,1)} %get-tuple-element.182, s32[]{:T(128)S(6)} %select_n.24, pred[6528]{0:T(1024)(128)(4,1)S(1)} %iota_compare_fusion.6, s32[512]{0:T(512)S(1)} %mul.129), kind=kOutput, calls=%fused_computation.51.clone.1 | convolution fusion | flops 872349184 | bytes 15182212 | tf_op jit(solution)/shard_map/while/body/eval_jaxpr/dot_general | solution.py:18
  43.1 2.1 fusion.53
  45.2 2.7 fusion.54
  47.9 0.6 dynamic_slice.29
  49.3 5.6 %fusion.52 = (f32[512]{0:T(512)S(1)}, f32[512,6528]{1,0:T(8,128)S(1)}) fusion(bf16[6528,128]{1,0:T(8,128)(2,1)} %get-tuple-element.183, bf16[512,1024]{1,0:T(8,128)(2,1)} %get-tuple-element.182, s32[]{:T(128)S(6)} %select_n.24, pred[6528]{0:T(1024)(128)(4,1)S(1)} %iota_compare_fusion.6, s32[512]{0:T(512)S(1)} %mul.129), kind=kOutput, calls=%fused_computation.51.clone.1 | convolution fusion | flops 872349184 | bytes 15182212 | tf_op jit(solution)/shard_map/while/body/eval_jaxpr/dot_general | solution.py:18
  54.9 2.1 fusion.53
  57.0 2.7 fusion.54
  59.7 0.6 dynamic_slice.29
  61.2 5.6 %fusion.52 = (f32[512]{0:T(512)S(1)}, f32[512,6528]{1,0:T(8,128)S(1)}) fusion(bf16[6528,128]{1,0:T(8,128)(2,1)} %get-tuple-element.183, bf16[512,1024]{1,0:T(8,128)(2,1)} %get-tuple-element.182, s32[]{:T(128)S(6)} %select_n.24, pred[6528]{0:T(1024)(128)(4,1)S(1)} %iota_compare_fusion.6, s32[512]{0:T(512)S(1)} %mul.129), kind=kOutput, calls=%fused_computation.51.clone.1 | convolution fusion | flops 872349184 | bytes 15182212 | tf_op jit(solution)/shard_map/while/body/eval_jaxpr/dot_general | solution.py:18
  66.8 2.1 fusion.53
  68.9 2.7 fusion.54
  71.6 0.6 dynamic_slice.29
  73.1 5.6 %fusion.52 = (f32[512]{0:T(512)S(1)}, f32[512,6528]{1,0:T(8,128)S(1)}) fusion(bf16[6528,128]{1,0:T(8,128)(2,1)} %get-tuple-element.183, bf16[512,1024]{1,0:T(8,128)(2,1)} %get-tuple-element.182, s32[]{:T(128)S(6)} %select_n.24, pred[6528]{0:T(1024)(128)(4,1)S(1)} %iota_compare_fusion.6, s32[512]{0:T(512)S(1)} %mul.129), kind=kOutput, calls=%fused_computation.51.clone.1 | convolution fusion | flops 872349184 | bytes 15182212 | tf_op jit(solution)/shard_map/while/body/eval_jaxpr/dot_general | solution.py:18
  78.7 2.1 fusion.53
  80.8 2.7 fusion.54
  83.5 0.6 dynamic_slice.29
  84.9 5.6 %fusion.52 = (f32[512]{0:T(512)S(1)}, f32[512,6528]{1,0:T(8,128)S(1)}) fusion(bf16[6528,128]{1,0:T(8,128)(2,1)} %get-tuple-element.183, bf16[512,1024]{1,0:T(8,128)(2,1)} %get-tuple-element.182, s32[]{:T(128)S(6)} %select_n.24, pred[6528]{0:T(1024)(128)(4,1)S(1)} %iota_compare_fusion.6, s32[512]{0:T(512)S(1)} %mul.129), kind=kOutput, calls=%fused_computation.51.clone.1 | convolution fusion | flops 872349184 | bytes 15182212 | tf_op jit(solution)/shard_map/while/body/eval_jaxpr/dot_general | solution.py:18
  90.6 2.1 fusion.53
  92.7 2.7 fusion.54
  95.3 0.6 dynamic_slice.29
  96.8 5.6 %fusion.52 = (f32[512]{0:T(512)S(1)}, f32[512,6528]{1,0:T(8,128)S(1)}) fusion(bf16[6528,128]{1,0:T(8,128)(2,1)} %get-tuple-element.183, bf16[512,1024]{1,0:T(8,128)(2,1)} %get-tuple-element.182, s32[]{:T(128)S(6)} %select_n.24, pred[6528]{0:T(1024)(128)(4,1)S(1)} %iota_compare_fusion.6, s32[512]{0:T(512)S(1)} %mul.129), kind=kOutput, calls=%fused_computation.51.clone.1 | convolution fusion | flops 872349184 | bytes 15182212 | tf_op jit(solution)/shard_map/while/body/eval_jaxpr/dot_general | solution.py:18
  102.4 2.1 fusion.53
  104.5 2.7 fusion.54
  107.2 0.6 dynamic_slice.29
  108.7 5.6 %fusion.52 = (f32[512]{0:T(512)S(1)}, f32[512,6528]{1,0:T(8,128)S(1)}) fusion(bf16[6528,128]{1,0:T(8,128)(2,1)} %get-tuple-element.183, bf16[512,1024]{1,0:T(8,128)(2,1)} %get-tuple-element.182, s32[]{:T(128)S(6)} %select_n.24, pred[6528]{0:T(1024)(128)(4,1)S(1)} %iota_compare_fusion.6, s32[512]{0:T(512)S(1)} %mul.129), kind=kOutput, calls=%fused_computation.51.clone.1 | convolution fusion | flops 872349184 | bytes 15182212 | tf_op jit(solution)/shard_map/while/body/eval_jaxpr/dot_general | solution.py:18
  114.3 2.1 fusion.53
  116.4 2.7 fusion.54
  119.1 0.6 dynamic_slice.29
  120.6 5.6 %fusion.52 = (f32[512]{0:T(512)S(1)}, f32[512,6528]{1,0:T(8,128)S(1)}) fusion(bf16[6528,128]{1,0:T(8,128)(2,1)} %get-tuple-element.183, bf16[512,1024]{1,0:T(8,128)(2,1)} %get-tuple-element.182, s32[]{:T(128)S(6)} %select_n.24, pred[6528]{0:T(1024)(128)(4,1)S(1)} %iota_compare_fusion.6, s32[512]{0:T(512)S(1)} %mul.129), kind=kOutput, calls=%fused_computation.51.clone.1 | convolution fusion | flops 872349184 | bytes 15182212 | tf_op jit(solution)/shard_map/while/body/eval_jaxpr/dot_general | solution.py:18
  126.2 2.1 fusion.53
  128.3 2.7 fusion.54
  131.0 2.0 copy.39
  133.4 19.1 %all_to_all.10 = bf16[16,2,16,1024]{3,2,1,0:T(8,128)(2,1)S(1)} all-to-all(bf16[16,2,16,1024]{3,2,1,0:T(8,128)(2,1)S(1)} %reshape.80), channel_id=1, replica_groups=mesh['seq'=16,'heads'=8] {'seq'}, dimensions={0} | all-to-all | bytes 2097152 | tf_op jit(solution)/shard_map/all_to_all | solution.py:85
  152.5 1.2 convolution_convert_fusion.1
  153.7 1.1 copy.41
  156.3 69.8 %all-gather.3.cloned.1.call-done = bf16[256,8192]{1,0:T(8,128)(2,1)} async-done(((bf16[256,1024]{1,0:T(8,128)(2,1)}), bf16[256,8192]{1,0:T(8,128)(2,1)}) %all-gather.3.cloned.1.call-update) | async-done | bytes 4194320 | tf_op jit(solution)/shard_map/all_gather | solution.py:93
  226.0 91.0 %all-gather.5.cloned.1.call-done = bf16[8192,1024]{1,0:T(8,128)(2,1)} async-done(((bf16[512,1024]{1,0:T(8,128)(2,1)}), bf16[8192,1024]{1,0:T(8,128)(2,1)}) %all-gather.5.cloned.1.call-update) | async-done | bytes 16777232 | tf_op jit(solution)/shard_map/all_gather | solution.py:96
  317.1 11.8 %fusion.24 = (f32[256]{0:T(256)S(1)}, f32[256]{0:T(256)S(1)}, bf16[256,1024]{1,0:T(8,128)(2,1)S(1)}) fusion(bf16[256,1024]{1,0:T(8,128)(2,1)S(1)} %copy-done.1, f32[1024]{0:T(1024)S(1)} %copy-done.4, bf16[256,8192]{1,0:T(8,128)(2,1)} %all-gather.3.cloned.1.call-done, bf16[8192,1024]{1,0:T(8,128)(2,1)} %all-gather.5.cloned.1.call-done, f32[]{:T(128)} %bitcast, ...), kind=kOutput, calls=%fused_computation.26 | convolution fusion | flops 4297850880 | bytes 22550532 | tf_op jit(solution)/shard_map/dot_general | solution.py:94
  328.9 24.4 %all-reduce = (f32[256]{0:T(256)S(1)}, f32[256]{0:T(256)S(1)}) all-reduce(f32[256]{0:T(256)S(1)} %get-tuple-element.73, f32[256]{0:T(256)S(1)} %get-tuple-element.72), channel_id=1, replica_groups=mesh['seq'=16,'heads'=8] {'heads'}, use_global_device_ids=true, to_apply=%region_10.11 | all-reduce | flops 512 | bytes 4096 | tf_op jit(solution)/shard_map/psum | solution.py:102
  353.4 1.3 fusion.26
  (59 shorter events, 5.0 us)
Async XLA Ops:
  7.2 1.1 copy-start
  7.2 10.0 %copy-start.5 = (s32[256]{0:T(256)S(1)}, s32[256]{0:T(256)}, u32[]{:S(2)}) copy-start(s32[256]{0:T(256)} %param.20) | copy-start | bytes 3076
  7.2 10.3 %copy-start.6 = (s32[16]{0:T(128)S(1)}, s32[16]{0:T(128)}, u32[]{:S(2)}) copy-start(s32[16]{0:T(128)} %param.18) | copy-start | bytes 196
  11.2 22.3 %all-to-all-start = ((bf16[16,2,16,1024]{3,1,2,0:T(2,128)(2,1)}), bf16[16,2,16,1024]{3,1,2,0:T(2,128)(2,1)}, u32[]{:S(2)}, u32[]{:S(2)}) async-start(bf16[16,2,16,1024]{3,1,2,0:T(2,128)(2,1)} %copy.36), calls=%async_computation | async-start | bytes 2097152 | tf_op jit(solution)/shard_map/all_to_all | solution.py:68
  16.9 209.1 %all-gather.3.cloned.1.call-start = ((), (), s32[]{:S(2)}) async-start(), calls=%async_computation.2 | async-start | bytes 4718592 | tf_op jit(solution)/shard_map/all_gather | solution.py:93
  131.0 186.1 %copy-start.1 = (bf16[256,1024]{1,0:T(8,128)(2,1)S(1)}, bf16[256,1024]{1,0:T(8,128)(2,1)}, u32[]{:S(2)}) copy-start(bf16[256,1024]{1,0:T(8,128)(2,1)} %param.22) | copy-start | bytes 1572868
  131.0 186.1 %copy-start.4 = (f32[1024]{0:T(1024)S(1)}, f32[1024]{0:T(1024)}, u32[]{:S(2)}) copy-start(f32[1024]{0:T(1024)} %param.21) | copy-start | bytes 12292
  154.8 162.2 %all-gather.5.cloned.1.call-start = ((), (), s32[]{:S(2)}) async-start(), calls=%async_computation.3 | async-start | bytes 17825792 | tf_op jit(solution)/shard_map/all_gather | solution.py:96
  317.1 36.3 %copy-start.2 = (bf16[256,1024]{1,0:T(8,128)(2,1)S(1)}, bf16[256,1024]{1,0:T(8,128)(2,1)}, u32[]{:S(2)}) copy-start(bf16[256,1024]{1,0:T(8,128)(2,1)} %param.23) | copy-start | bytes 1572868
  328.9 25.7 %copy-start.3 = (bf16[256,1024]{1,0:T(8,128)(2,1)}, bf16[256,1024]{1,0:T(8,128)(2,1)S(1)}, u32[]{:S(2)}) copy-start(bf16[256,1024]{1,0:T(8,128)(2,1)S(1)} %get-tuple-element.100) | copy-start | bytes 1572868
Sparse Core Ops, SparseCore 0:
  155.0 71.0 all-gather.2
  227.8 89.2 all-gather.4
where the time goes:
time: 362 us; the launch traced here: 361 us
  waiting for transfers between devices  173 us (48%)
  matrix products  80 us (22%)
  blocking collectives  43.5 us (12%)
  local copies, waits for them, and re-layouts  19.9 us (5%)
  other arithmetic  18.7 us (5%)
  between operations  15.4 us (4%)
  starting transfers between devices  5.93 us (2%)
  loops' own time  5.21 us (1%)
    all_gather x1, waiting for transfers between devices, local(): lax.all_gather(out_weight, 'seq', axis=0, tiled=True)  91 us
    all_gather x1, waiting for transfers between devices, local(): full_context = lax.all_gather(context, 'heads', axis=1, tiled=True)  69.8 us
    dot_general x8, matrix products, head_scores(): lax.dot_general(query_head, key_block, (((1,), (1,)), ((), ())), preferre...  44.9 us
    psum x1, blocking collectives, local(): lax.psum((jnp.sum(hidden * hidden, axis=1), jnp.sum(hidden * scaled, axis...  24.4 us
    dot_general x8, matrix products, one_head(): jnp.dot(probs.astype(jnp.bfloat16), values_here, preferred_element_type=j...  21.5 us
    all_to_all x1, blocking collectives, local(): lax.all_to_all(merged, 'seq', split_axis=0, concat_axis=0, tiled=True)  19.1 us
    reduce_sum x8, other arithmetic, one_head(): total = jnp.sum(probs, axis=1, keepdims=True)  16.8 us
    dot_general x1, matrix products, local(): jnp.dot(full_context, lax.all_gather(out_weight, 'seq', axis=0, tiled=Tru...  11.8 us
  transfers between devices with their start and end apart: 3, of which 3 were waited for; matrix products, arithmetic and copies ran while one was open for 1% of the time, Pallas kernels for 0%

commit v1 on v0

--- a/solution.py
+++ b/solution.py
@@ -90,7 +90,9 @@
         preferred_element_type=jnp.float32,
     )
     context = context.astype(jnp.bfloat16).reshape(tok_rows, q_width)
-    full_context = lax.all_gather(context, "heads", axis=1, tiled=True)
+    full_context = jnp.concatenate(
+        lax.all_to_all(jnp.stack([context] * lax.axis_size("heads")), "heads", 0, 0), axis=1
+    )
     branch = jnp.dot(
         full_context,
         lax.all_gather(out_weight, "seq", axis=0, tiled=True),

time: 362 us -> 267 us (0.74)
  waiting for transfers between devices: 173 us -> 71.1 us
  starting transfers between devices: 5.93 us -> 14.3 us
  blocking collectives: 43.5 us -> 39.5 us
    all_gather x1, waiting for transfers between devices: 91 us -> 0.01 us  [local(): lax.all_gather(out_weight, 'seq', axis=0, tiled=True)]
    all_gather x1 -> x0, waiting for transfers between devices: 69.8 us -> none  [local(): full_context = lax.all_gather(context, 'heads', axis=1, tiled=True)]
    all_to_all x0 -> x1, waiting for transfers between devices: none -> 49.8 us  [local(): lax.all_to_all(jnp.stack([context] * lax.axis_size('heads')), 'heads', 0, 0)]
    all_to_all x1, waiting for transfers between devices: 11.6 us -> 20.6 us  [local(): lax.all_to_all(outgoing, 'seq', split_axis=0, concat_axis=0, tiled=True)]
    all_to_all x0 -> x1, starting transfers between devices: none -> 8.63 us  [local(): lax.all_to_all(jnp.stack([context] * lax.axis_size('heads')), 'heads', 0, 0)]
    psum x1, blocking collectives: 24.4 us -> 20.5 us  [local(): lax.psum((jnp.sum(hidden * hidden, axis=1), jnp.sum(hidden * scaled, axis...]
  transfers between devices with their start and end apart: 3 -> 3, of which waited for: 3 -> 2; matrix products, arithmetic and copies ran while one was open for 1% -> 40% of each run, Pallas kernels for 0% -> 0%
where the time goes in v1:
time: 267 us
  matrix products  80.2 us (30%)
  waiting for transfers between devices  71.1 us (27%)
  blocking collectives  39.5 us (15%)
  local copies, waits for them, and re-layouts  21.7 us (8%)
  other arithmetic  18.7 us (7%)
  between operations  15.5 us (6%)
  starting transfers between devices  14.3 us (5%)
  loops' own time  5.68 us (2%)
    all_to_all x1, waiting for transfers between devices, local(): lax.all_to_all(jnp.stack([context] * lax.axis_size('heads')), 'heads', 0, 0)  49.8 us
    dot_general x8, matrix products, head_scores(): lax.dot_general(query_head, key_block, (((1,), (1,)), ((), ())), preferre...  45.1 us
    dot_general x8, matrix products, one_head(): jnp.dot(probs.astype(jnp.bfloat16), values_here, preferred_element_type=j...  21.5 us
    all_to_all x1, waiting for transfers between devices, local(): lax.all_to_all(outgoing, 'seq', split_axis=0, concat_axis=0, tiled=True)  20.6 us
    psum x1, blocking collectives, local(): lax.psum((jnp.sum(hidden * hidden, axis=1), jnp.sum(hidden * scaled, axis...  20.5 us
    all_to_all x1, blocking collectives, local(): lax.all_to_all(merged, 'seq', split_axis=0, concat_axis=0, tiled=True)  19.1 us
    reduce_sum x8, other arithmetic, one_head(): total = jnp.sum(probs, axis=1, keepdims=True)  16.8 us
    dot_general x1, matrix products, local(): jnp.dot(full_context, lax.all_gather(out_weight, 'seq', axis=0, tiled=Tru...  11.9 us
  transfers between devices with their start and end apart: 3, of which 2 were waited for; matrix products, arithmetic and copies ran while one was open for 40% of the time, Pallas kernels for 0%

profile of v1, /device:TPU:0, one launch (start us, length us, event | category | flops | bytes accessed | tf_op | source)
XLA Modules:
  0.0 266.6 jit_solution(3042900136336205248)
XLA Ops:
  7.2 0.7 all-gather.2.cloned.1.call-update
  7.9 0.8 reshape.81
  9.9 2.0 copy.39
  11.9 5.7 %all-to-all-start = ((bf16[16,2,16,1024]{3,1,2,0:T(2,128)(2,1)}), bf16[16,2,16,1024]{3,1,2,0:T(2,128)(2,1)}, u32[]{:S(2)}, u32[]{:S(2)}) async-start(bf16[16,2,16,1024]{3,1,2,0:T(2,128)(2,1)} %copy.39), calls=%async_computation | async-start | bytes 2097152 | tf_op jit(solution)/shard_map/all_to_all | solution.py:68
  19.3 3.4 %slice_bitcast_fusion = (bf16[6528,128]{1,0:T(8,128)(2,1)S(1)}, bf16[6528,128]{1,0:T(8,128)(2,1)}) fusion(bf16[1,2,6528,128]{3,2,1,0:T(8,128)(2,1)} %param.15), kind=kLoop, calls=%fused_computation.16 | loop fusion | bytes 6684672 | tf_op jit(solution)/shard_map/squeeze | solution.py:67
  22.6 20.6 %all-to-all-done = bf16[16,2,16,1024]{3,1,2,0:T(2,128)(2,1)} async-done(((bf16[16,2,16,1024]{3,1,2,0:T(2,128)(2,1)}), bf16[16,2,16,1024]{3,1,2,0:T(2,128)(2,1)}, u32[]{:S(2)}, u32[]{:S(2)}) %all-to-all-start) | async-done | bytes 1048608 | tf_op jit(solution)/shard_map/all_to_all | solution.py:68
  43.3 2.5 copy.40
  45.8 95.8 %while.11 = (s32[]{:T(128)}, bf16[8,512,128]{2,1,0:T(8,128)(2,1)}, s32[]{:T(128)}, s32[8]{0:T(128)S(1)}, bf16[512,1024]{1,0:T(8,128)(2,1)}, /*index=5*/bf16[6528...) while((s32[]{:T(128)}, bf16[8,512,128]{2,1,0:T(8,128)(2,1)}, ...), condition=%wide.region_6.7_spmd.clone, body=%wide.region_3.6_spmd.clone.sunk | while | flops 1741493632 | bytes 43744824 | solution.py:83
  45.8 0.7 dynamic_slice.29
  47.3 5.6 %fusion.52 = (f32[512]{0:T(512)S(1)}, f32[512,6528]{1,0:T(8,128)S(1)}) fusion(bf16[6528,128]{1,0:T(8,128)(2,1)} %get-tuple-element.183, bf16[512,1024]{1,0:T(8,128)(2,1)} %get-tuple-element.182, s32[]{:T(128)S(6)} %select_n.24, pred[6528]{0:T(1024)(128)(4,1)S(1)} %iota_compare_fusion.6, s32[512]{0:T(512)S(1)} %mul.129), kind=kOutput, calls=%fused_computation.51.clone.1 | convolution fusion | flops 872349184 | bytes 15182212 | tf_op jit(solution)/shard_map/while/body/eval_jaxpr/dot_general | solution.py:18
  53.0 2.1 fusion.53
  55.1 2.7 %fusion.54 = bf16[8,512,128]{2,1,0:T(8,128)(2,1)} fusion(bf16[8,512,128]{2,1,0:T(8,128)(2,1)} %get-tuple-element.167, s32[]{:T(128)} %get-tuple-element.166, bf16[6528,128]{1,0:T(8,128)(2,1)S(1)} %get-tuple-element.184, f32[512,6528]{1,0:T(8,128)S(1)} %get-tuple-element.152, f32[512]{0:T(512)S(1)} %get-tuple-element.153, f32[512]{0:T(512)S(1)} %fusion.53), kind=kOutput, calls=%fused_computation.12.clone.1 | convolution fusion | flops 862453760 | bytes 15176192 | tf_op jit(solution)/shard_map/while/body/eval_jaxpr/dot_general | solution.py:80
  57.7 0.7 dynamic_slice.29
  59.3 5.6 %fusion.52 = (f32[512]{0:T(512)S(1)}, f32[512,6528]{1,0:T(8,128)S(1)}) fusion(bf16[6528,128]{1,0:T(8,128)(2,1)} %get-tuple-element.183, bf16[512,1024]{1,0:T(8,128)(2,1)} %get-tuple-element.182, s32[]{:T(128)S(6)} %select_n.24, pred[6528]{0:T(1024)(128)(4,1)S(1)} %iota_compare_fusion.6, s32[512]{0:T(512)S(1)} %mul.129), kind=kOutput, calls=%fused_computation.51.clone.1 | convolution fusion | flops 872349184 | bytes 15182212 | tf_op jit(solution)/shard_map/while/body/eval_jaxpr/dot_general | solution.py:18
  64.9 2.1 fusion.53
  67.0 2.7 %fusion.54 = bf16[8,512,128]{2,1,0:T(8,128)(2,1)} fusion(bf16[8,512,128]{2,1,0:T(8,128)(2,1)} %get-tuple-element.167, s32[]{:T(128)} %get-tuple-element.166, bf16[6528,128]{1,0:T(8,128)(2,1)S(1)} %get-tuple-element.184, f32[512,6528]{1,0:T(8,128)S(1)} %get-tuple-element.152, f32[512]{0:T(512)S(1)} %get-tuple-element.153, f32[512]{0:T(512)S(1)} %fusion.53), kind=kOutput, calls=%fused_computation.12.clone.1 | convolution fusion | flops 862453760 | bytes 15176192 | tf_op jit(solution)/shard_map/while/body/eval_jaxpr/dot_general | solution.py:80
  69.7 0.7 dynamic_slice.29
  71.2 5.7 %fusion.52 = (f32[512]{0:T(512)S(1)}, f32[512,6528]{1,0:T(8,128)S(1)}) fusion(bf16[6528,128]{1,0:T(8,128)(2,1)} %get-tuple-element.183, bf16[512,1024]{1,0:T(8,128)(2,1)} %get-tuple-element.182, s32[]{:T(128)S(6)} %select_n.24, pred[6528]{0:T(1024)(128)(4,1)S(1)} %iota_compare_fusion.6, s32[512]{0:T(512)S(1)} %mul.129), kind=kOutput, calls=%fused_computation.51.clone.1 | convolution fusion | flops 872349184 | bytes 15182212 | tf_op jit(solution)/shard_map/while/body/eval_jaxpr/dot_general | solution.py:18
  77.0 2.1 fusion.53
  79.1 2.7 %fusion.54 = bf16[8,512,128]{2,1,0:T(8,128)(2,1)} fusion(bf16[8,512,128]{2,1,0:T(8,128)(2,1)} %get-tuple-element.167, s32[]{:T(128)} %get-tuple-element.166, bf16[6528,128]{1,0:T(8,128)(2,1)S(1)} %get-tuple-element.184, f32[512,6528]{1,0:T(8,128)S(1)} %get-tuple-element.152, f32[512]{0:T(512)S(1)} %get-tuple-element.153, f32[512]{0:T(512)S(1)} %fusion.53), kind=kOutput, calls=%fused_computation.12.clone.1 | convolution fusion | flops 862453760 | bytes 15176192 | tf_op jit(solution)/shard_map/while/body/eval_jaxpr/dot_general | solution.py:80
  81.8 0.7 dynamic_slice.29
  83.3 5.6 %fusion.52 = (f32[512]{0:T(512)S(1)}, f32[512,6528]{1,0:T(8,128)S(1)}) fusion(bf16[6528,128]{1,0:T(8,128)(2,1)} %get-tuple-element.183, bf16[512,1024]{1,0:T(8,128)(2,1)} %get-tuple-element.182, s32[]{:T(128)S(6)} %select_n.24, pred[6528]{0:T(1024)(128)(4,1)S(1)} %iota_compare_fusion.6, s32[512]{0:T(512)S(1)} %mul.129), kind=kOutput, calls=%fused_computation.51.clone.1 | convolution fusion | flops 872349184 | bytes 15182212 | tf_op jit(solution)/shard_map/while/body/eval_jaxpr/dot_general | solution.py:18
  89.0 2.1 fusion.53
  91.1 2.7 %fusion.54 = bf16[8,512,128]{2,1,0:T(8,128)(2,1)} fusion(bf16[8,512,128]{2,1,0:T(8,128)(2,1)} %get-tuple-element.167, s32[]{:T(128)} %get-tuple-element.166, bf16[6528,128]{1,0:T(8,128)(2,1)S(1)} %get-tuple-element.184, f32[512,6528]{1,0:T(8,128)S(1)} %get-tuple-element.152, f32[512]{0:T(512)S(1)} %get-tuple-element.153, f32[512]{0:T(512)S(1)} %fusion.53), kind=kOutput, calls=%fused_computation.12.clone.1 | convolution fusion | flops 862453760 | bytes 15176192 | tf_op jit(solution)/shard_map/while/body/eval_jaxpr/dot_general | solution.py:80
  93.7 0.7 dynamic_slice.29
  95.3 5.6 %fusion.52 = (f32[512]{0:T(512)S(1)}, f32[512,6528]{1,0:T(8,128)S(1)}) fusion(bf16[6528,128]{1,0:T(8,128)(2,1)} %get-tuple-element.183, bf16[512,1024]{1,0:T(8,128)(2,1)} %get-tuple-element.182, s32[]{:T(128)S(6)} %select_n.24, pred[6528]{0:T(1024)(128)(4,1)S(1)} %iota_compare_fusion.6, s32[512]{0:T(512)S(1)} %mul.129), kind=kOutput, calls=%fused_computation.51.clone.1 | convolution fusion | flops 872349184 | bytes 15182212 | tf_op jit(solution)/shard_map/while/body/eval_jaxpr/dot_general | solution.py:18
  100.9 2.1 fusion.53
  103.0 2.7 %fusion.54 = bf16[8,512,128]{2,1,0:T(8,128)(2,1)} fusion(bf16[8,512,128]{2,1,0:T(8,128)(2,1)} %get-tuple-element.167, s32[]{:T(128)} %get-tuple-element.166, bf16[6528,128]{1,0:T(8,128)(2,1)S(1)} %get-tuple-element.184, f32[512,6528]{1,0:T(8,128)S(1)} %get-tuple-element.152, f32[512]{0:T(512)S(1)} %get-tuple-element.153, f32[512]{0:T(512)S(1)} %fusion.53), kind=kOutput, calls=%fused_computation.12.clone.1 | convolution fusion | flops 862453760 | bytes 15176192 | tf_op jit(solution)/shard_map/while/body/eval_jaxpr/dot_general | solution.py:80
  105.7 0.7 dynamic_slice.29
  107.3 5.6 %fusion.52 = (f32[512]{0:T(512)S(1)}, f32[512,6528]{1,0:T(8,128)S(1)}) fusion(bf16[6528,128]{1,0:T(8,128)(2,1)} %get-tuple-element.183, bf16[512,1024]{1,0:T(8,128)(2,1)} %get-tuple-element.182, s32[]{:T(128)S(6)} %select_n.24, pred[6528]{0:T(1024)(128)(4,1)S(1)} %iota_compare_fusion.6, s32[512]{0:T(512)S(1)} %mul.129), kind=kOutput, calls=%fused_computation.51.clone.1 | convolution fusion | flops 872349184 | bytes 15182212 | tf_op jit(solution)/shard_map/while/body/eval_jaxpr/dot_general | solution.py:18
  112.9 2.1 fusion.53
  115.0 2.7 %fusion.54 = bf16[8,512,128]{2,1,0:T(8,128)(2,1)} fusion(bf16[8,512,128]{2,1,0:T(8,128)(2,1)} %get-tuple-element.167, s32[]{:T(128)} %get-tuple-element.166, bf16[6528,128]{1,0:T(8,128)(2,1)S(1)} %get-tuple-element.184, f32[512,6528]{1,0:T(8,128)S(1)} %get-tuple-element.152, f32[512]{0:T(512)S(1)} %get-tuple-element.153, f32[512]{0:T(512)S(1)} %fusion.53), kind=kOutput, calls=%fused_computation.12.clone.1 | convolution fusion | flops 862453760 | bytes 15176192 | tf_op jit(solution)/shard_map/while/body/eval_jaxpr/dot_general | solution.py:80
  117.7 0.7 dynamic_slice.29
  119.2 5.6 %fusion.52 = (f32[512]{0:T(512)S(1)}, f32[512,6528]{1,0:T(8,128)S(1)}) fusion(bf16[6528,128]{1,0:T(8,128)(2,1)} %get-tuple-element.183, bf16[512,1024]{1,0:T(8,128)(2,1)} %get-tuple-element.182, s32[]{:T(128)S(6)} %select_n.24, pred[6528]{0:T(1024)(128)(4,1)S(1)} %iota_compare_fusion.6, s32[512]{0:T(512)S(1)} %mul.129), kind=kOutput, calls=%fused_computation.51.clone.1 | convolution fusion | flops 872349184 | bytes 15182212 | tf_op jit(solution)/shard_map/while/body/eval_jaxpr/dot_general | solution.py:18
  124.8 2.1 fusion.53
  126.9 2.7 %fusion.54 = bf16[8,512,128]{2,1,0:T(8,128)(2,1)} fusion(bf16[8,512,128]{2,1,0:T(8,128)(2,1)} %get-tuple-element.167, s32[]{:T(128)} %get-tuple-element.166, bf16[6528,128]{1,0:T(8,128)(2,1)S(1)} %get-tuple-element.184, f32[512,6528]{1,0:T(8,128)S(1)} %get-tuple-element.152, f32[512]{0:T(512)S(1)} %get-tuple-element.153, f32[512]{0:T(512)S(1)} %fusion.53), kind=kOutput, calls=%fused_computation.12.clone.1 | convolution fusion | flops 862453760 | bytes 15176192 | tf_op jit(solution)/shard_map/while/body/eval_jaxpr/dot_general | solution.py:80
  131.2 5.6 %fusion.52 = (f32[512]{0:T(512)S(1)}, f32[512,6528]{1,0:T(8,128)S(1)}) fusion(bf16[6528,128]{1,0:T(8,128)(2,1)} %get-tuple-element.183, bf16[512,1024]{1,0:T(8,128)(2,1)} %get-tuple-element.182, s32[]{:T(128)S(6)} %select_n.24, pred[6528]{0:T(1024)(128)(4,1)S(1)} %iota_compare_fusion.6, s32[512]{0:T(512)S(1)} %mul.129), kind=kOutput, calls=%fused_computation.51.clone.1 | convolution fusion | flops 872349184 | bytes 15182212 | tf_op jit(solution)/shard_map/while/body/eval_jaxpr/dot_general | solution.py:18
  136.8 2.1 fusion.53
  138.9 2.7 %fusion.54 = bf16[8,512,128]{2,1,0:T(8,128)(2,1)} fusion(bf16[8,512,128]{2,1,0:T(8,128)(2,1)} %get-tuple-element.167, s32[]{:T(128)} %get-tuple-element.166, bf16[6528,128]{1,0:T(8,128)(2,1)S(1)} %get-tuple-element.184, f32[512,6528]{1,0:T(8,128)S(1)} %get-tuple-element.152, f32[512]{0:T(512)S(1)} %get-tuple-element.153, f32[512]{0:T(512)S(1)} %fusion.53), kind=kOutput, calls=%fused_computation.12.clone.1 | convolution fusion | flops 862453760 | bytes 15176192 | tf_op jit(solution)/shard_map/while/body/eval_jaxpr/dot_general | solution.py:80
  141.6 1.9 copy.42
  144.0 19.1 %all_to_all.15 = bf16[16,2,16,1024]{3,2,1,0:T(8,128)(2,1)S(1)} all-to-all(bf16[16,2,16,1024]{3,2,1,0:T(8,128)(2,1)S(1)} %reshape.85), channel_id=1, replica_groups=mesh['seq'=16,'heads'=8] {'seq'}, dimensions={0} | all-to-all | bytes 2097152 | tf_op jit(solution)/shard_map/all_to_all | solution.py:85
  163.0 1.2 convolution_convert_fusion.1
  164.8 2.2 stack.3
  167.0 8.6 %all-to-all-start.2 = ((bf16[8,256,1024]{1,2,0:T(8,128)(2,1)}), bf16[8,256,1024]{1,2,0:T(8,128)(2,1)}, u32[]{:S(2)}, u32[]{:S(2)}) async-start(bf16[8,256,1024]{1,2,0:T(8,128)(2,1)} %stack.3), calls=%async_computation.2 | async-start | bytes 8388608 | tf_op jit(solution)/shard_map/all_to_all | solution.py:94
  176.3 49.8 %all-to-all-done.2 = bf16[8,256,1024]{1,2,0:T(8,128)(2,1)} async-done(((bf16[8,256,1024]{1,2,0:T(8,128)(2,1)}), bf16[8,256,1024]{1,2,0:T(8,128)(2,1)}, u32[]{:S(2)}, u32[]{:S(2)}) %all-to-all-start.2) | async-done | bytes 4194336 | tf_op jit(solution)/shard_map/all_to_all | solution.py:94
  226.2 11.9 %fusion.24 = (f32[256]{0:T(256)S(1)}, f32[256]{0:T(256)S(1)}, bf16[256,1024]{1,0:T(8,128)(2,1)S(1)}) fusion(bf16[256,1024]{1,0:T(8,128)(2,1)S(1)} %copy-done.1, f32[1024]{0:T(1024)S(1)} %copy-done.5, bf16[256,8192]{0,1:T(8,128)(2,1)} %bitcast.12, bf16[8192,1024]{1,0:T(8,128)(2,1)} %all-gather.2.cloned.1.call-done, f32[]{:T(128)} %bitcast, ...), kind=kOutput, calls=%fused_computation.26 | convolution fusion | flops 4297850880 | bytes 22550532 | tf_op jit(solution)/shard_map/dot_general | solution.py:96
  238.0 20.5 %all-reduce = (f32[256]{0:T(256)S(1)}, f32[256]{0:T(256)S(1)}) all-reduce(f32[256]{0:T(256)S(1)} %get-tuple-element.73, f32[256]{0:T(256)S(1)} %get-tuple-element.72), channel_id=1, replica_groups=mesh['seq'=16,'heads'=8] {'heads'}, use_global_device_ids=true, to_apply=%region_10.11 | all-reduce | flops 512 | bytes 4096 | tf_op jit(solution)/shard_map/psum | solution.py:104
  258.5 1.3 fusion.26
  (62 shorter events, 5.5 us)
Async XLA Ops:
  7.2 1.7 copy-start
  7.2 10.6 %copy-start.6 = (s32[256]{0:T(256)S(1)}, s32[256]{0:T(256)}, u32[]{:S(2)}) copy-start(s32[256]{0:T(256)} %param.20) | copy-start | bytes 3076
  7.2 10.9 %copy-start.7 = (s32[16]{0:T(128)S(1)}, s32[16]{0:T(128)}, u32[]{:S(2)}) copy-start(s32[16]{0:T(128)} %param.18) | copy-start | bytes 196
  7.2 218.9 %all-gather.2.cloned.1.call-start = ((), (), s32[]{:S(2)}) async-start(), calls=%async_computation.3 | async-start | bytes 17825792 | tf_op jit(solution)/shard_map/all_gather | solution.py:98
  11.9 31.3 %all-to-all-start = ((bf16[16,2,16,1024]{3,1,2,0:T(2,128)(2,1)}), bf16[16,2,16,1024]{3,1,2,0:T(2,128)(2,1)}, u32[]{:S(2)}, u32[]{:S(2)}) async-start(bf16[16,2,16,1024]{3,1,2,0:T(2,128)(2,1)} %copy.39), calls=%async_computation | async-start | bytes 2097152 | tf_op jit(solution)/shard_map/all_to_all | solution.py:68
  164.8 61.4 %copy-start.1 = (bf16[256,1024]{1,0:T(8,128)(2,1)S(1)}, bf16[256,1024]{1,0:T(8,128)(2,1)}, u32[]{:S(2)}) copy-start(bf16[256,1024]{1,0:T(8,128)(2,1)} %param.22) | copy-start | bytes 1572868
  164.8 61.4 %copy-start.3 = (bf16[256,1024]{1,0:T(8,128)(2,1)S(1)}, bf16[256,1024]{1,0:T(8,128)(2,1)}, u32[]{:S(2)}) copy-start(bf16[256,1024]{1,0:T(8,128)(2,1)} %param.13) | copy-start | bytes 1572868
  164.8 61.4 %copy-start.5 = (f32[1024]{0:T(1024)S(1)}, f32[1024]{0:T(1024)}, u32[]{:S(2)}) copy-start(f32[1024]{0:T(1024)} %param.21) | copy-start | bytes 12292
  167.0 59.1 %all-to-all-start.2 = ((bf16[8,256,1024]{1,2,0:T(8,128)(2,1)}), bf16[8,256,1024]{1,2,0:T(8,128)(2,1)}, u32[]{:S(2)}, u32[]{:S(2)}) async-start(bf16[8,256,1024]{1,2,0:T(8,128)(2,1)} %stack.3), calls=%async_computation.2 | async-start | bytes 8388608 | tf_op jit(solution)/shard_map/all_to_all | solution.py:94
  226.1 32.4 %copy-start.4 = (bf16[256,1024]{1,0:T(8,128)(2,1)S(1)}, bf16[256,1024]{1,0:T(8,128)(2,1)}, u32[]{:S(2)}) copy-start(bf16[256,1024]{1,0:T(8,128)(2,1)} %param.23) | copy-start | bytes 1572868
  238.0 21.8 %copy-start.2 = (bf16[256,1024]{1,0:T(8,128)(2,1)}, bf16[256,1024]{1,0:T(8,128)(2,1)S(1)}, u32[]{:S(2)}) copy-start(bf16[256,1024]{1,0:T(8,128)(2,1)S(1)} %get-tuple-element.100) | copy-start | bytes 1572868
Sparse Core Ops, SparseCore 0:
  9.7 102.6 all-gather.1
